TPU v7x, 32 devices: a whole 2x2x4 slice. The times are simulated.
32 devices in a mesh: lat: 4 (over y, x), lon: 8 (over z, core).
Axes of the slice: x: 2, y: 2, z: 4, core: 2. Of those that a mesh axis runs over, the one named last changes fastest.
Arguments:
- fields: bfloat16 [1, 64, 64, 768], P(None, 'lat', 'lon'), may hold values from -6 to 6
- spec_cotangent: bfloat16 [2, 1, 64, 32, 768], P(None, None, 'lon', 'lat'), may hold values from -6 to 6
- inner_kernel: bfloat16 [2, 8, 96, 96], replicated, may hold values from -0.4375 to 0.4375
- inner_offset: float32 [2, 8, 96], replicated, may hold values from -3 to 3
- outer_kernel: bfloat16 [2, 8, 96, 96], replicated, may hold values from -0.4375 to 0.4375
- outer_offset: float32 [2, 8, 96], replicated, may hold values from -3 to 3
Outputs:
- filtered: float32 [2, 1, 64, 32, 768], P(None, None, 'lon', 'lat')
- inner_kernel_grad: float32 [2, 8, 96, 96], replicated
- inner_offset_grad: float32 [2, 8, 96], replicated
- outer_kernel_grad: float32 [2, 8, 96, 96], replicated
- outer_offset_grad: float32 [2, 8, 96], replicated
All inputs are finite; a program needn't handle non-finite values.
Results may differ from a plain program's by a relative error of at most 0.0072.
Values may be sent and summed in bfloat16 or wider, within the bound.
A program may use at most 64 MiB of HBM per device.

v0:
```python
import math

import jax
import jax.numpy as jnp
from jax import lax
from jax.sharding import PartitionSpec as P

shrink_level = 0.1
gelu_coeff = 0.7978845608028654
precise = lax.Precision.HIGHEST


def dft_tables(length, columns):
    points = jnp.arange(length, dtype=jnp.int32)
    orders = jnp.arange(columns, dtype=jnp.int32)
    product = points[:, None] * orders[None, :] % length
    angles = product.astype(jnp.float32) * (2.0 * math.pi / length)
    factor = 1.0 / math.sqrt(length)
    return (jnp.cos(angles) * factor, jnp.sin(angles) * factor)


def shrink(values):
    return values - shrink_level * jnp.tanh(values / shrink_level)


def shrink_slope(values):
    level = jnp.tanh(values / shrink_level)
    return level * level


def gelu_value(values):
    inner = gelu_coeff * (values + 0.044715 * values * values * values)
    return 0.5 * values * (1.0 + jnp.tanh(inner))


def gelu_slope(values):
    inner = gelu_coeff * (values + 0.044715 * values * values * values)
    level = jnp.tanh(inner)
    return 0.5 * (1.0 + level) + 0.5 * values * (1.0 - level * level) * gelu_coeff * (
        1.0 + 3.0 * 0.044715 * values * values
    )


def mixing(operand, kernel):
    return jnp.einsum("rnb,nbc->rnc", operand, kernel, preferred_element_type=jnp.float32)


def backmix(operand, kernel):
    return jnp.einsum("rnc,nbc->rnb", operand, kernel, preferred_element_type=jnp.float32)


def crossed(operand, second):
    return jnp.einsum("rnb,rnc->nbc", operand, second, preferred_element_type=jnp.float32)


def block_filter(spectrum, cotangent, inner_kernel, inner_offset, outer_kernel, outer_offset):
    spec_real, spec_imag = (spectrum[0], spectrum[1])
    pre_real = (
        mixing(spec_real, inner_kernel[0]) - mixing(spec_imag, inner_kernel[1]) + inner_offset[0]
    )
    pre_imag = (
        mixing(spec_imag, inner_kernel[0]) + mixing(spec_real, inner_kernel[1]) + inner_offset[1]
    )
    hid_real = gelu_value(pre_real).astype(jnp.bfloat16)
    hid_imag = gelu_value(pre_imag).astype(jnp.bfloat16)
    out_real = (
        mixing(hid_real, outer_kernel[0]) - mixing(hid_imag, outer_kernel[1]) + outer_offset[0]
    )
    out_imag = (
        mixing(hid_imag, outer_kernel[0]) + mixing(hid_real, outer_kernel[1]) + outer_offset[1]
    )
    filtered = jnp.stack([shrink(out_real), shrink(out_imag)])
    back_real = (cotangent[0].astype(jnp.float32) * shrink_slope(out_real)).astype(jnp.bfloat16)
    back_imag = (cotangent[1].astype(jnp.float32) * shrink_slope(out_imag)).astype(jnp.bfloat16)
    outer_grad = jnp.stack(
        [
            crossed(hid_real, back_real) + crossed(hid_imag, back_imag),
            crossed(hid_real, back_imag) - crossed(hid_imag, back_real),
        ]
    )
    outer_bias = jnp.stack(
        [
            jnp.sum(back_real, axis=0, dtype=jnp.float32),
            jnp.sum(back_imag, axis=0, dtype=jnp.float32),
        ]
    )
    grad_real = (
        (backmix(back_real, outer_kernel[0]) + backmix(back_imag, outer_kernel[1]))
        * gelu_slope(pre_real)
    ).astype(jnp.bfloat16)
    grad_imag = (
        (backmix(back_imag, outer_kernel[0]) - backmix(back_real, outer_kernel[1]))
        * gelu_slope(pre_imag)
    ).astype(jnp.bfloat16)
    inner_grad = jnp.stack(
        [
            crossed(spec_real, grad_real) + crossed(spec_imag, grad_imag),
            crossed(spec_real, grad_imag) - crossed(spec_imag, grad_real),
        ]
    )
    inner_bias = jnp.stack(
        [
            jnp.sum(grad_real, axis=0, dtype=jnp.float32),
            jnp.sum(grad_imag, axis=0, dtype=jnp.float32),
        ]
    )
    return (filtered, (inner_grad, inner_bias, outer_grad, outer_bias))


def per_device(fields, spec_cotangent, inner_kernel, inner_offset, outer_kernel, outer_offset):
    lat_devices = lax.axis_size("lat")
    lon_devices = lax.axis_size("lon")
    conditions = fields.shape[0]
    height = fields.shape[1] * lat_devices
    width = fields.shape[2] * lon_devices
    wavenumbers = width // 2
    cosine_rows, sine_rows = dft_tables(height, height)
    cosine_cols, sine_cols = dft_tables(width, wavenumbers)
    arriving = lax.all_to_all(fields, "lat", split_axis=3, concat_axis=1, tiled=True)
    shape_in = arriving.shape
    floats = arriving.astype(jnp.float32).reshape(
        shape_in[0], shape_in[1], shape_in[2] * shape_in[3]
    )
    real_part = jnp.einsum("bhx,hm->bmx", floats, cosine_rows, precision=precise)
    imag_part = -jnp.einsum("bhx,hm->bmx", floats, sine_rows, precision=precise)
    spec_rows = jnp.stack([real_part, imag_part]).reshape((2,) + shape_in)
    arriving = lax.all_to_all(spec_rows, "lon", split_axis=2, concat_axis=3, tiled=True)
    real_part = jnp.einsum(
        "bhwd,wk->bhkd", arriving[0], cosine_cols, precision=precise
    ) + jnp.einsum("bhwd,wk->bhkd", arriving[1], sine_cols, precision=precise)
    imag_part = jnp.einsum(
        "bhwd,wk->bhkd", arriving[1], cosine_cols, precision=precise
    ) - jnp.einsum("bhwd,wk->bhkd", arriving[0], sine_cols, precision=precise)
    spec_half = jnp.stack([real_part, imag_part]).astype(jnp.bfloat16)
    spectrum = lax.all_to_all(spec_half, "lat", split_axis=3, concat_axis=4, tiled=True)
    blocks = inner_kernel.shape[1]
    block_width = inner_kernel.shape[2]
    local_shape = spectrum.shape
    flat_spec = spectrum.reshape(2, -1, blocks, block_width)
    flat_cot = spec_cotangent.reshape(2, -1, blocks, block_width)
    filtered, gradients = block_filter(
        flat_spec, flat_cot, inner_kernel, inner_offset, outer_kernel, outer_offset
    )
    totals = lax.psum((gradients[0], gradients[1], gradients[2], gradients[3]), ("lat", "lon"))
    normalizer = 1.0 / math.sqrt(conditions * height * wavenumbers)
    return (
        filtered.reshape(local_shape),
        totals[0] * normalizer,
        totals[1] * normalizer,
        totals[2] * normalizer,
        totals[3] * normalizer,
    )


def solution(mesh):
    placed = (P(None, "lat", "lon", None), P(None, None, "lon", "lat", None), P(), P(), P(), P())
    return jax.shard_map(
        per_device,
        mesh=mesh,
        in_specs=placed,
        out_specs=(P(None, None, "lon", "lat", None), P(), P(), P(), P()),
        check_vma=False,
    )
```

profile of v0, /device:TPU:0, one launch (start us, length us, event | category | flops | bytes accessed | tf_op | source)
XLA Modules:
  0.0 218.2 jit_solution(6437234970947821318)
XLA Ops:
  7.2 2.2 copy.51
  9.3 1.6 reshape.124
  10.9 10.5 %all_to_all.45 = bf16[4,2,12288]{2,1,0:T(2,128)(2,1)S(1)} all-to-all(bf16[4,2,12288]{2,1,0:T(2,128)(2,1)S(1)} %reshape.124), channel_id=1, replica_groups=mesh['lat'=4,'lon'=8] {'lat'}, dimensions={0} | all-to-all | bytes 393216 | tf_op jit(solution)/shard_map/all_to_all | solution.py:119
  21.4 1.2 reshape.125
  22.6 1.0 copy.52
  23.6 0.2 reshape.116
  23.9 0.4 convolution_negate_fusion
  24.3 0.2 dot_general.85
  24.5 0.5 convolution_bitcast_fusion
  25.0 0.2 stack.60
  25.2 0.2 copy.54
  25.4 0.1 pad_maximum_fusion
  25.5 1.6 copy.55
  27.1 5.0 %all-to-all-start.1 = ((f32[2,1,64,8,192]{4,3,1,0,2:T(8,128)}), f32[2,1,64,8,192]{4,3,1,0,2:T(8,128)S(1)}, u32[]{:S(2)}, u32[]{:S(2)}) async-start(f32[2,1,64,8,192]{4,3,1,0,2:T(8,128)} %copy.55), calls=%async_computation.1 | async-start | bytes 2097152 | tf_op jit(solution)/shard_map/all_to_all | solution.py:127
  32.1 0.1 reshape.119
  32.2 0.1 reshape.120
  32.4 26.3 %all-to-all-done.1 = f32[2,1,64,8,192]{4,3,1,0,2:T(8,128)S(1)} async-done(((f32[2,1,64,8,192]{4,3,1,0,2:T(8,128)}), f32[2,1,64,8,192]{4,3,1,0,2:T(8,128)S(1)}, u32[]{:S(2)}, u32[]{:S(2)}) %all-to-all-start.1) | async-done | bytes 786464 | tf_op jit(solution)/shard_map/all_to_all | solution.py:127
  58.7 0.1 copy.103
  58.8 0.5 fusion.23
  59.2 0.5 fusion.22
  59.7 0.0 copy-start.4
  59.7 0.5 fusion.20
  60.2 0.5 fusion.21
  60.6 0.0 copy-start.1
  60.7 0.9 copy.57
  61.6 3.4 %all-to-all-start.2 = ((bf16[2,1,8,32,192]{4,2,1,0,3:T(8,128)(2,1)}), bf16[2,1,8,32,192]{4,2,1,0,3:T(8,128)(2,1)S(1)}, u32[]{:S(2)}, u32[]{:S(2)}) async-start(bf16[2,1,8,32,192]{4,2,1,0,3:T(8,128)(2,1)} %copy.57), calls=%async_computation.2 | async-start | bytes 524288 | tf_op jit(solution)/shard_map/all_to_all | solution.py:135
  65.0 0.2 all-reduce.4.cloned.1.call-start
  65.2 5.2 %all-to-all-done.2 = bf16[2,1,8,32,192]{4,2,1,0,3:T(8,128)(2,1)S(1)} async-done(((bf16[2,1,8,32,192]{4,2,1,0,3:T(8,128)(2,1)}), bf16[2,1,8,32,192]{4,2,1,0,3:T(8,128)(2,1)S(1)}, u32[]{:S(2)}, u32[]{:S(2)}) %all-to-all-start.2) | async-done | bytes 196640 | tf_op jit(solution)/shard_map/all_to_all | solution.py:135
  70.4 0.2 copy.104
  70.6 0.1 fusion.142
  70.7 0.1 squeeze.12
  70.9 0.1 squeeze.14
  71.0 0.2 fusion.51
  71.2 0.2 fusion.53
  71.4 0.3 multiply_convert_fusion
  71.7 0.2 fusion.45
  71.9 0.3 multiply_convert_fusion.1
  72.1 0.2 fusion.47
  72.3 0.3 convert_reduce_fusion.1
  72.6 0.2 fusion.43
  72.8 0.3 fusion.143
  73.1 0.3 convert_reduce_fusion
  73.4 0.2 fusion.41
  73.6 0.3 fusion.144
  73.9 0.3 convert_reduce_fusion.3
  74.2 0.2 fusion.73
  74.5 0.3 convert_reduce_fusion.2
  74.8 0.2 fusion.71
  75.0 0.3 fusion.3
  75.3 0.3 fusion.2
  75.5 0.3 fusion.1
  75.8 0.3 fusion
  76.1 0.9 pad_maximum_fusion.1
  77.0 0.9 pad_maximum_fusion.2
  78.0 0.0 all-reduce.4.cloned.1.call-update
  78.0 0.2 copy.64
  78.2 0.1 stack.66
  78.3 0.2 copy.63
  78.4 0.1 stack.65
  78.6 37.5 %all-reduce = (f32[2,8,96]{2,1,0:T(8,128)S(1)}, f32[2,8,96]{2,1,0:T(8,128)S(1)}) all-reduce(f32[2,8,96]{2,1,0:T(8,128)S(1)} %pad_maximum_fusion.5, f32[2,8,96]{2,1,0:T(8,128)S(1)} %pad_maximum_fusion.6), channel_id=1, replica_groups=mesh['lat'=4,'lon'=8] {'lat','lon'}, use_global_device_ids=true, to_apply=%region_3.4 | all-reduce | flops 3072 | bytes 24576 | tf_op jit(solution)/shard_map/psum | solution.py:144
  116.1 0.8 pad_maximum_fusion.3
  116.9 0.6 broadcast_multiply_fusion.2
  117.5 91.3 %all-reduce.4.cloned.1.call-done = (f32[2,8,96,96]{3,2,1,0:T(8,128)}, f32[2,8,96,96]{3,2,1,0:T(8,128)}) async-done(((f32[2,8,96,96]{3,2,1,0:T(8,128)}, f32[2,8,96,96]{3,2,1,0:T(8,128)}), (f32[2,8,96,96]{3,2,1,0:T(8,128)}, f32[2,8,96,96]{3,2,1,0:T(8,128)})) %all-reduce.4.cloned.1.call-update) | async-done | bytes 1179664 | tf_op jit(solution)/shard_map/psum | solution.py:144
  208.7 2.7 %broadcast_multiply_fusion = (f32[2,8,96,96]{3,2,1,0:T(8,128)}, f32[2,8,96,96]{3,2,1,0:T(8,128)}) fusion(f32[2,8,96,96]{3,2,1,0:T(8,128)} %get-tuple-element.8, f32[2,8,96,96]{3,2,1,0:T(8,128)} %get-tuple-element.7), kind=kLoop, calls=%fused_computation.45 | loop fusion | flops 294912 | bytes 2359296 | tf_op jit(solution)/shard_map/mul | solution.py:150
  (14 shorter events, 0.1 us)
Async XLA Ops:
  27.0 5.0 %copy-start.2 = (bf16[2,1,8,8,768]{4,3,2,1,0:T(8,128)(2,1)S(1)}, bf16[2,1,8,8,768]{4,3,2,1,0:T(8,128)(2,1)}, u32[]{:S(2)}) copy-start(bf16[2,1,8,8,768]{4,3,2,1,0:T(8,128)(2,1)} %param.7) | copy-start | bytes 589828
  27.1 5.3 %copy-start.3 = (f32[2,8,96]{2,1,0:T(8,128)S(1)}, f32[2,8,96]{2,1,0:T(8,128)}, u32[]{:S(2)}) copy-start(f32[2,8,96]{2,1,0:T(8,128)} %param.9) | copy-start | bytes 18436
  27.1 31.6 %all-to-all-start.1 = ((f32[2,1,64,8,192]{4,3,1,0,2:T(8,128)}), f32[2,1,64,8,192]{4,3,1,0,2:T(8,128)S(1)}, u32[]{:S(2)}, u32[]{:S(2)}) async-start(f32[2,1,64,8,192]{4,3,1,0,2:T(8,128)} %copy.55), calls=%async_computation.1 | async-start | bytes 2097152 | tf_op jit(solution)/shard_map/all_to_all | solution.py:127
  59.7 5.5 %copy-start.4 = (f32[2,8,96]{2,1,0:T(8,128)S(1)}, f32[2,8,96]{2,1,0:T(8,128)}, u32[]{:S(2)}) copy-start(f32[2,8,96]{2,1,0:T(8,128)} %param.11) | copy-start | bytes 18436
  60.6 10.4 %copy-start.1 = (bf16[2,8,96,96]{3,2,1,0:T(8,128)(2,1)S(1)}, bf16[2,8,96,96]{3,2,1,0:T(8,128)(2,1)}, u32[]{:S(2)}) copy-start(bf16[2,8,96,96]{3,2,1,0:T(8,128)(2,1)} %param.8) | copy-start | bytes 884740
  61.6 8.8 %all-to-all-start.2 = ((bf16[2,1,8,32,192]{4,2,1,0,3:T(8,128)(2,1)}), bf16[2,1,8,32,192]{4,2,1,0,3:T(8,128)(2,1)S(1)}, u32[]{:S(2)}, u32[]{:S(2)}) async-start(bf16[2,1,8,32,192]{4,2,1,0,3:T(8,128)(2,1)} %copy.57), calls=%async_computation.2 | async-start | bytes 524288 | tf_op jit(solution)/shard_map/all_to_all | solution.py:135
  65.0 143.8 %all-reduce.4.cloned.1.call-start = ((), (), s32[]{:S(2)}) async-start(), calls=%async_computation.3 | async-start | bytes 3145728 | tf_op jit(solution)/shard_map/psum | solution.py:144
  70.6 1.1 copy-start
Sparse Core Ops, SparseCore 0:
  78.1 130.5 all-reduce.3
where the time goes:
time: 219 us; the launch traced here: 218 us
  waiting for transfers between devices  123 us (56%)
  blocking collectives  48 us (22%)
  between operations  14.4 us (7%)
  local copies, waits for them, and re-layouts  10.7 us (5%)
  starting transfers between devices  8.63 us (4%)
  matrix products  7.71 us (4%)
  other arithmetic  6.09 us (3%)
    psum x1, waiting for transfers between devices, per_device(): lax.psum((gradients[0], gradients[1], gradients[2], gradients[3]), ('lat'...  91.3 us
    psum x1, blocking collectives, per_device(): lax.psum((gradients[0], gradients[1], gradients[2], gradients[3]), ('lat'...  37.5 us
    all_to_all x1, waiting for transfers between devices, per_device(): lax.all_to_all(spec_rows, 'lon', split_axis=2, concat_axis=3, tiled=True)  26.3 us
    all_to_all x1, blocking collectives, per_device(): lax.all_to_all(fields, 'lat', split_axis=3, concat_axis=1, tiled=True)  10.5 us
    all_to_all x1, waiting for transfers between devices, per_device(): lax.all_to_all(spec_half, 'lat', split_axis=3, concat_axis=4, tiled=True)  5.17 us
    all_to_all x1, starting transfers between devices, per_device(): lax.all_to_all(spec_rows, 'lon', split_axis=2, concat_axis=3, tiled=True)  5 us
    unnamed x13, local copies, waits for them, and re-layouts  4.92 us
  transfers between devices with their start and end apart: 3, of which 3 were waited for; matrix products, arithmetic and copies ran while one was open for 1% of the time, Pallas kernels for 0%

commit v1 on v0

--- a/solution.py
+++ b/solution.py
@@ -2,7 +2,10 @@
 
 import jax
 import jax.numpy as jnp
+import numpy as np
 from jax import lax
+from jax.experimental import pallas as pl
+from jax.experimental.pallas import tpu as pltpu
 from jax.sharding import PartitionSpec as P
 
 shrink_level = 0.1
@@ -152,10 +155,442 @@
     )
 
 
+def split_table(table):
+    high = table.astype(jnp.bfloat16)
+    low = (table - high.astype(np.float64)).astype(jnp.bfloat16)
+    return np.stack([high, low])
+
+
+def phase_tables(length, columns):
+    product = np.arange(length)[:, None] * np.arange(columns)[None, :] % length
+    angles = product * (2.0 * math.pi / length)
+    return np.cos(angles) / math.sqrt(length), np.sin(angles) / math.sqrt(length)
+
+
+def column_tables(width, wavenumbers, groups):
+    cosine, sine = phase_tables(width, wavenumbers)
+    both = np.stack([cosine.T, -sine.T]).reshape(2, groups, wavenumbers // groups, width)
+    return split_table(both.transpose(1, 0, 2, 3).reshape(2 * wavenumbers, width))
+
+
+def row_tables(height, inner):
+    cosine, sine = phase_tables(height, height)
+    eye = np.eye(inner)
+    both = np.stack([np.kron(cosine.T, eye), np.kron(sine.T, eye)])
+    return split_table(both)
+
+
+def padded(values, lanes):
+    rows, columns = values.shape
+    return jnp.concatenate([values, jnp.zeros((rows, lanes - columns), values.dtype)], axis=1)
+
+
+def fused_kernel(
+    sizes,
+    fields_ref,
+    cot_ref,
+    inner_ref,
+    inner_off_ref,
+    outer_ref,
+    outer_off_ref,
+    cols_ref,
+    rows_hbm,
+    filt_ref,
+    inner_grad_ref,
+    outer_grad_ref,
+    bias_ref,
+    send_a,
+    recv_a,
+    send_b,
+    recv_b,
+    send_c,
+    recv_c,
+    send_d,
+    recv_d,
+    send_e,
+    recv_e,
+    gather,
+    spec_s,
+    hid_s,
+    back_s,
+    hb_s,
+    raw_w,
+    w1,
+    w2,
+    rows_ref,
+    lon_send,
+    lon_recv,
+    lat_send,
+    lat_recv,
+    core_send,
+    core_recv,
+    local_sem,
+):
+    lats, lons, blocks, width, lanes, normalizer = sizes
+    i = lax.axis_index("lat")
+    j = lax.axis_index("lon")
+    h_local, w_local, _ = fields_ref.shape
+    m_local, k_local = cot_ref.shape[1], cot_ref.shape[2]
+    tokens = spec_s.shape[0]
+    part_rows = m_local * k_local
+    zs = lons // 2
+    f32, bf16 = jnp.float32, jnp.bfloat16
+
+    loads = [pltpu.make_async_copy(rows_hbm, rows_ref, local_sem.at[0])]
+    for p in range(2):
+        loads.append(
+            pltpu.make_async_copy(inner_ref.at[p, j], raw_w.at[p], local_sem.at[1 + p])
+        )
+        loads.append(
+            pltpu.make_async_copy(outer_ref.at[p, j], raw_w.at[2 + p], local_sem.at[3 + p])
+        )
+    for load in loads:
+        load.start()
+
+    barrier = pltpu.get_barrier_semaphore()
+
+    def greet_lon(d, carry):
+        pl.semaphore_signal(
+            barrier, inc=1, device_id=(i, lax.rem(j + d, lons)), device_id_type=pl.DeviceIdType.MESH
+        )
+        return carry
+
+    def greet_lat(d, carry):
+        pl.semaphore_signal(
+            barrier, inc=1, device_id=(lax.rem(i + d, lats), j), device_id_type=pl.DeviceIdType.MESH
+        )
+        return carry
+
+    lax.fori_loop(1, lons, greet_lon, 0)
+    lax.fori_loop(1, lats, greet_lat, 0)
+
+    for h in range(h_local):
+        row = fields_ref[h].astype(f32)
+        for b in range(blocks):
+            send_a[b, :, h * lanes : (h + 1) * lanes] = padded(
+                row[:, b * width : (b + 1) * width], lanes
+            ).astype(bf16)
+
+    pl.semaphore_wait(barrier, lons + lats - 2)
+
+    def lon_copy(phase, src, dst, d):
+        return pltpu.make_async_remote_copy(
+            src_ref=src,
+            dst_ref=dst,
+            send_sem=lon_send.at[phase, d],
+            recv_sem=lon_recv.at[phase, d],
+            device_id=(i, lax.rem(j + d, lons)),
+            device_id_type=pl.DeviceIdType.MESH,
+        )
+
+    def lat_copy(phase, src, dst, d):
+        return pltpu.make_async_remote_copy(
+            src_ref=src,
+            dst_ref=dst,
+            send_sem=lat_send.at[phase, d],
+            recv_sem=lat_recv.at[phase, d],
+            device_id=(lax.rem(i + d, lats), j),
+            device_id_type=pl.DeviceIdType.MESH,
+        )
+
+    def exchange_start(copy, phase, send, recv, me, n):
+        def one(d, carry):
+            copy(phase, send.at[lax.rem(me + d, n)], recv.at[me], d).start()
+            return carry
+
+        lax.fori_loop(1, n, one, 0)
+
+    def exchange_recv(copy, phase, send, recv, me, n):
+        def one(d, carry):
+            source = lax.rem(me + n - d, n)
+            copy(phase, send.at[source], recv.at[source], d).wait_recv()
+            return carry
+
+        lax.fori_loop(1, n, one, 0)
+
+    def exchange_sent(copy, phase, send, recv, me, n):
+        def one(d, carry):
+            copy(phase, send.at[lax.rem(me + d, n)], recv.at[me], d).wait_send()
+            return carry
+
+        lax.fori_loop(1, n, one, 0)
+
+    exchange_start(lon_copy, 0, send_a, recv_a, j, lons)
+    recv_a[j] = send_a[j]
+
+    for p in range(2):
+        part = jnp.concatenate([cot_ref[p, m].astype(f32) for m in range(m_local)], axis=0)
+        for b in range(blocks):
+            send_c[b, :, p * lanes : (p + 1) * lanes] = padded(
+                part[:, b * width : (b + 1) * width], lanes
+            ).astype(bf16)
+    exchange_start(lon_copy, 1, send_c, recv_c, j, lons)
+    recv_c[j] = send_c[j]
+
+    for load in loads[1:]:
+        load.wait()
+    w1[...] = jnp.zeros_like(w1)
+    w2[...] = jnp.zeros_like(w2)
+    for target, base in ((w1, 0), (w2, 2)):
+        real, imag = raw_w[base], raw_w[base + 1]
+        target[0:width, 0:width] = real
+        target[0:width, lanes : lanes + width] = imag
+        target[lanes : lanes + width, 0:width] = -imag
+        target[lanes : lanes + width, lanes : lanes + width] = real
+    off1 = jnp.concatenate(
+        [padded(inner_off_ref[p, pl.ds(j, 1), :], lanes) for p in range(2)], axis=1
+    )
+    off2 = jnp.concatenate(
+        [padded(outer_off_ref[p, pl.ds(j, 1), :], lanes) for p in range(2)], axis=1
+    )
+    loads[0].wait()
+
+    exchange_recv(lon_copy, 0, send_a, recv_a, j, lons)
+    columns = jnp.concatenate([recv_a[s].astype(f32) for s in range(lons)], axis=0).astype(bf16)
+    half = jnp.dot(cols_ref[0], columns, preferred_element_type=f32) + jnp.dot(
+        cols_ref[1], columns, preferred_element_type=f32
+    )
+    for g in range(lats):
+        for p in range(2):
+            first = (2 * g + p) * k_local
+            send_b[g, :, p * lanes : (p + 1) * lanes] = jnp.concatenate(
+                [
+                    half[first : first + k_local, h * lanes : (h + 1) * lanes]
+                    for h in range(h_local)
+                ],
+                axis=0,
+            ).astype(bf16)
+    exchange_start(lat_copy, 0, send_b, recv_b, i, lats)
+    recv_b[i] = send_b[i]
+    exchange_recv(lon_copy, 1, send_c, recv_c, j, lons)
+    exchange_recv(lat_copy, 0, send_b, recv_b, i, lats)
+
+    chunks = 4
+    chunk = tokens // chunks
+    per_chunk = lons // chunks
+    lane = lax.broadcasted_iota(jnp.int32, (chunk, 2 * lanes), 1)
+    ones_lane = lane == width
+    one = jnp.ones((chunk, 2 * lanes), f32)
+
+    def block_layers(c, carry):
+        rows = pl.ds(pl.multiple_of(c * chunk, chunk), chunk)
+        lines = recv_b[...].reshape(tokens, 2 * lanes)
+        cos_part = jnp.dot(rows_ref[0, 0, rows, :], lines, preferred_element_type=f32) + jnp.dot(
+            rows_ref[1, 0, rows, :], lines, preferred_element_type=f32
+        )
+        sin_part = jnp.dot(rows_ref[0, 1, rows, :], lines, preferred_element_type=f32) + jnp.dot(
+            rows_ref[1, 1, rows, :], lines, preferred_element_type=f32
+        )
+        real = cos_part[:, :lanes] + sin_part[:, lanes:]
+        imag = cos_part[:, lanes:] - sin_part[:, :lanes]
+        spec_wide = jnp.concatenate([real, imag], axis=1)
+        spec = spec_wide.astype(bf16)
+        spec_s[rows, :] = jnp.where(ones_lane, one, spec_wide).astype(bf16)
+        pre = jnp.dot(spec, w1[...], preferred_element_type=f32) + off1
+        square = pre * pre
+        level = jnp.tanh(gelu_coeff * (pre + 0.044715 * pre * square))
+        hid_wide = 0.5 * pre * (1.0 + level)
+        slope = 0.5 * (1.0 + level) + 0.5 * pre * (1.0 - level * level) * gelu_coeff * (
+            1.0 + 3.0 * 0.044715 * square
+        )
+        hid_s[rows, :] = jnp.where(ones_lane, one, hid_wide).astype(bf16)
+        out = jnp.dot(hid_wide.astype(bf16), w2[...], preferred_element_type=f32) + off2
+        soft = jnp.tanh(out * (1.0 / shrink_level))
+        filtered = (out - shrink_level * soft).astype(bf16)
+        send_d[pl.ds(c * per_chunk, per_chunk)] = filtered.reshape(
+            per_chunk, part_rows, 2 * lanes
+        )
+        cot = recv_c[pl.ds(c * per_chunk, per_chunk)].reshape(chunk, 2 * lanes).astype(f32)
+        back = (cot * (soft * soft)).astype(bf16)
+        back_s[rows, :] = back
+        turned = lax.dot_general(
+            back, w2[...], (((1,), (1,)), ((), ())), preferred_element_type=f32
+        )
+        hb_s[rows, :] = (turned * slope).astype(bf16)
+        return carry
+
+    lax.fori_loop(0, chunks, block_layers, 0)
+    exchange_start(lon_copy, 2, send_d, recv_d, j, lons)
+    recv_d[j] = send_d[j]
+
+    deep = send_e.shape[1]
+    for base, left, right in ((2, hid_s, back_s), (0, spec_s, hb_s)):
+        full = lax.dot_general(
+            left[...], right[...], (((0,), (0,)), ((), ())), preferred_element_type=f32
+        )
+        send_e[base] = (full[0:deep, :lanes] + full[lanes : lanes + deep, lanes:]).astype(bf16)
+        send_e[base + 1] = (full[0:deep, lanes:] - full[lanes : lanes + deep, :lanes]).astype(bf16)
+    exchange_start(lat_copy, 1, send_e, recv_e, i, lats)
+    recv_e[i] = send_e[i]
+    exchange_recv(lat_copy, 1, send_e, recv_e, i, lats)
+    total = recv_e[0].astype(f32)
+    for s in range(1, lats):
+        total = total + recv_e[s].astype(f32)
+    side = lax.rem(j, 2)
+    z = lax.div(j, 2)
+    gather[side, i, z] = (total * normalizer).astype(bf16)
+
+    def z_copy(d, slot):
+        return pltpu.make_async_remote_copy(
+            src_ref=gather.at[side, i, slot],
+            dst_ref=gather.at[side, i, slot],
+            send_sem=lon_send.at[3, d],
+            recv_sem=lon_recv.at[3, d],
+            device_id=(i, lax.rem(j + 2 * d, lons)),
+            device_id_type=pl.DeviceIdType.MESH,
+        )
+
+    def side_copy(from_side, slot):
+        return pltpu.make_async_remote_copy(
+            src_ref=gather.at[from_side, slot],
+            dst_ref=gather.at[from_side, slot],
+            send_sem=core_send.at[slot],
+            recv_sem=core_recv.at[slot],
+            device_id=(i, j + 1 - 2 * side),
+            device_id_type=pl.DeviceIdType.MESH,
+        )
+
+    for d in range(1, zs):
+        z_copy(d, z).start()
+
+    exchange_recv(lon_copy, 2, send_d, recv_d, j, lons)
+    for p in range(2):
+        filt_ref[p] = jnp.concatenate(
+            [recv_d[b, :, p * lanes : p * lanes + width].astype(f32) for b in range(blocks)],
+            axis=1,
+        ).astype(bf16)
+
+    for d in range(1, zs):
+        z_copy(d, lax.rem(z + zs - d, zs)).wait_recv()
+    for d in range(1, lats):
+        lat_copy(2, gather.at[side, i], gather.at[side, i], d).start()
+    side_copy(side, i).start()
+    for d in range(1, lats):
+        source = lax.rem(i + lats - d, lats)
+        lat_copy(2, gather.at[side, source], gather.at[side, source], d).wait_recv()
+        side_copy(side, source).start()
+    other = 1 - side
+    for q in range(lats):
+        side_copy(other, q).wait_recv()
+
+    for q in range(lats):
+        target = inner_grad_ref if q < 2 else outer_grad_ref
+        for b in range(blocks):
+            piece = gather[b % 2, q, b // 2]
+            target[q % 2, b] = piece[0:width, 0:width]
+            bias_ref[q, b : b + 1, :] = piece[width:deep, 0:width].astype(f32)[0:1]
+
+    exchange_sent(lon_copy, 0, send_a, recv_a, j, lons)
+    exchange_sent(lon_copy, 1, send_c, recv_c, j, lons)
+    exchange_sent(lon_copy, 2, send_d, recv_d, j, lons)
+    exchange_sent(lat_copy, 0, send_b, recv_b, i, lats)
+    exchange_sent(lat_copy, 1, send_e, recv_e, i, lats)
+    for d in range(1, zs):
+        z_copy(d, z).wait_send()
+    for d in range(1, lats):
+        lat_copy(2, gather.at[side, i], gather.at[side, i], d).wait_send()
+    for q in range(lats):
+        side_copy(side, q).wait_send()
+
+
+def fused_device(fields, spec_cotangent, inner_kernel, inner_offset, outer_kernel, outer_offset):
+    lats = lax.axis_size("lat")
+    lons = lax.axis_size("lon")
+    _, h_local, w_local, channels = fields.shape
+    m_local, k_local = spec_cotangent.shape[2:4]
+    blocks, width = inner_kernel.shape[1:3]
+    height, full_width = h_local * lats, w_local * lons
+    wavenumbers = k_local * lats
+    lanes = 128
+    tokens = height * k_local
+    part_rows = m_local * k_local
+    deep = (width // 16 + 1) * 16
+    normalizer = 1.0 / math.sqrt(height * wavenumbers)
+    cols = jnp.asarray(column_tables(full_width, wavenumbers, lats))
+    rows = jnp.asarray(row_tables(height, k_local))
+    vmem = pl.BlockSpec(memory_space=pltpu.VMEM)
+    hbm = pl.BlockSpec(memory_space=pl.ANY)
+    bf16 = jnp.bfloat16
+    wide = (tokens, 2 * lanes)
+    dma = pltpu.SemaphoreType.DMA
+
+    def pair(*shape):
+        return [pltpu.VMEM(shape, bf16)] * 2
+
+    filt, inner_grad, outer_grad, bias = pl.pallas_call(
+        lambda *refs: fused_kernel((lats, lons, blocks, width, lanes, normalizer), *refs),
+        name="fused_filter",
+        out_shape=[
+            jax.ShapeDtypeStruct((2, part_rows, channels), bf16),
+            jax.ShapeDtypeStruct(inner_kernel.shape, bf16),
+            jax.ShapeDtypeStruct(outer_kernel.shape, bf16),
+            jax.ShapeDtypeStruct((4, blocks, width), jnp.float32),
+        ],
+        in_specs=[vmem, vmem, hbm, vmem, hbm, vmem, vmem, hbm],
+        out_specs=[vmem] * 4,
+        scratch_shapes=[
+            *pair(blocks, w_local, h_local * lanes),
+            *pair(lats, h_local * k_local, 2 * lanes),
+            *pair(blocks, part_rows, 2 * lanes),
+            *pair(blocks, part_rows, 2 * lanes),
+            *pair(4, deep, lanes),
+            pltpu.VMEM((2, lats, lons // 2, deep, lanes), bf16),
+            *[pltpu.VMEM(wide, bf16)] * 4,
+            pltpu.VMEM((4, width, width), bf16),
+            *pair(2 * lanes, 2 * lanes),
+            pltpu.VMEM(rows.shape, bf16),
+            dma((4, lons)),
+            dma((4, lons)),
+            dma((3, lats)),
+            dma((3, lats)),
+            dma((lats,)),
+            dma((lats,)),
+            dma((5,)),
+        ],
+        compiler_params=pltpu.CompilerParams(
+            collective_id=0, has_side_effects=True, vmem_limit_bytes=40 * 1024 * 1024
+        ),
+    )(
+        fields.reshape(fields.shape[1:]),
+        spec_cotangent.reshape(2, m_local, k_local, channels),
+        inner_kernel,
+        inner_offset,
+        outer_kernel,
+        outer_offset,
+        cols,
+        rows,
+    )
+    return (
+        filt.astype(jnp.float32).reshape(spec_cotangent.shape),
+        inner_grad.astype(jnp.float32),
+        bias[0:2],
+        outer_grad.astype(jnp.float32),
+        bias[2:4],
+    )
+
+
+def choose_device(fields, spec_cotangent, inner_kernel, *rest):
+    lats, lons = lax.axis_size("lat"), lax.axis_size("lon")
+    blocks, width = inner_kernel.shape[1:3]
+    fits = (
+        fields.shape[0] == 1
+        and lons == blocks
+        and lats == 4
+        and width % 16 == 0
+        and width < 128
+        and fields.shape[1] == 16
+        and fields.shape[2] == 8
+        and spec_cotangent.shape[2] == 8
+        and spec_cotangent.shape[3] == 8
+    )
+    chosen = fused_device if fits else per_device
+    return chosen(fields, spec_cotangent, inner_kernel, *rest)
+
+
 def solution(mesh):
     placed = (P(None, "lat", "lon", None), P(None, None, "lon", "lat", None), P(), P(), P(), P())
     return jax.shard_map(
-        per_device,
+        choose_device,
         mesh=mesh,
         in_specs=placed,
         out_specs=(P(None, None, "lon", "lat", None), P(), P(), P(), P()),

time: 219 us -> 51.3 us (0.23)
  waiting for transfers between devices: 123 us -> 0 us
  blocking collectives: 48 us -> 0 us
  Pallas kernels: 0 us -> 39 us
  between operations: 14.4 us -> 0.66 us
  starting transfers between devices: 8.63 us -> 0 us
  matrix products: 7.71 us -> 0 us
  other arithmetic: 6.09 us -> 2.69 us
  local copies, waits for them, and re-layouts: 10.7 us -> 8.19 us
    psum x1 -> x0, waiting for transfers between devices: 91.3 us -> none  [per_device(): lax.psum((gradients[0], gradients[1], gradients[2], gradients[3]), ('lat'...]
    pallas_call x0 -> x1, Pallas kernels: none -> 39 us  [fused_device(): pl.pallas_call(lambda *refs: fused_kernel((lats, lons, blocks, width, lan...]
    psum x1 -> x0, blocking collectives: 37.5 us -> none  [per_device(): lax.psum((gradients[0], gradients[1], gradients[2], gradients[3]), ('lat'...]
    all_to_all x2 -> x0, waiting for transfers between devices: 31.4 us -> none  [the longest x1 26.3 us: per_device(): lax.all_to_all(spec_rows, 'lon', split_axis=2, concat_axis=3, tiled=True)]
    all_to_all x1 -> x0, blocking collectives: 10.5 us -> none  [per_device(): lax.all_to_all(fields, 'lat', split_axis=3, concat_axis=1, tiled=True)]
    all_to_all x2 -> x0, starting transfers between devices: 8.41 us -> none  [the longest x1 5 us: per_device(): lax.all_to_all(spec_rows, 'lon', split_axis=2, concat_axis=3, tiled=True)]
    dot_general x26 -> x0, matrix products: 7.71 us -> none  [the longest x8 2.06 us: crossed(): jnp.einsum('rnb,rnc->nbc', operand, second, preferred_element_type=jnp.fl...]
    mul x2 -> x0, other arithmetic: 3.26 us -> none  [the longest x1 2.65 us: per_device(): totals[2] * normalizer]
  transfers between devices with their start and end apart: 3 -> 0, of which waited for: 3 -> 0; matrix products, arithmetic and copies ran while one was open for 1% -> 0% of each run, Pallas kernels for 0% -> 0%
where the time goes in v1:
time: 51.3 us; the launch traced here: 50.5 us
  Pallas kernels  39 us (76%)
  local copies, waits for them, and re-layouts  8.19 us (16%)
  other arithmetic  2.69 us (5%)
  between operations  0.66 us (1%)
    pallas_call x1, Pallas kernels, fused_device(): pl.pallas_call(lambda *refs: fused_kernel((lats, lons, blocks, width, lan...  39 us
    unnamed x16, local copies, waits for them, and re-layouts  7.58 us

profile of v1, /device:TPU:0, one launch (start us, length us, event | category | flops | bytes accessed | tf_op | source)
XLA Modules:
  0.0 50.5 jit_solution(15552293921202290368)
XLA Ops:
  0.6 0.0 copy-start
  0.6 1.6 %copy-done = bf16[2,2,512,512]{3,2,1,0:T(8,128)(2,1)S(1)} copy-done((bf16[2,2,512,512]{3,2,1,0:T(8,128)(2,1)S(1)}, bf16[2,2,512,512]{3,2,1,0:T(8,128)(2,1)}, u32[]{:S(2)}) %copy-start) | copy-done | bytes 2097176
  2.2 0.0 copy-start.1
  2.2 1.0 %copy-done.1 = bf16[2,8,96,96]{3,2,1,0:T(8,128)(2,1)S(1)} copy-done((bf16[2,8,96,96]{3,2,1,0:T(8,128)(2,1)S(1)}, bf16[2,8,96,96]{3,2,1,0:T(8,128)(2,1)}, u32[]{:S(2)}) %copy-start.1) | copy-done | bytes 294936
  3.2 0.0 copy-start.2
  3.2 1.0 %copy-done.2 = bf16[2,8,96,96]{3,2,1,0:T(8,128)(2,1)S(1)} copy-done((bf16[2,8,96,96]{3,2,1,0:T(8,128)(2,1)S(1)}, bf16[2,8,96,96]{3,2,1,0:T(8,128)(2,1)}, u32[]{:S(2)}) %copy-start.2) | copy-done | bytes 294936
  4.2 0.0 copy-start.3
  4.2 0.9 %copy-done.3 = bf16[1,16,8,768]{3,2,1,0:T(8,128)(2,1)S(1)} copy-done((bf16[1,16,8,768]{3,2,1,0:T(8,128)(2,1)S(1)}, bf16[1,16,8,768]{3,2,1,0:T(8,128)(2,1)}, u32[]{:S(2)}) %copy-start.3) | copy-done | bytes 196632
  5.1 0.0 copy-start.4
  5.2 0.9 %copy-done.4 = bf16[2,1,8,8,768]{4,3,2,1,0:T(8,128)(2,1)S(1)} copy-done((bf16[2,1,8,8,768]{4,3,2,1,0:T(8,128)(2,1)S(1)}, bf16[2,1,8,8,768]{4,3,2,1,0:T(8,128)(2,1)}, u32[]{:S(2)}) %copy-start.4) | copy-done | bytes 196632
  6.1 0.0 copy-start.5
  6.1 0.8 %copy-done.5 = bf16[2,64,64]{2,1,0:T(8,128)(2,1)S(1)} copy-done((bf16[2,64,64]{2,1,0:T(8,128)(2,1)S(1)}, bf16[2,64,64]{2,1,0:T(8,128)(2,1)}, u32[]{:S(2)}) %copy-start.5) | copy-done | bytes 16408
  6.8 0.0 copy-start.6
  6.8 0.7 %copy-done.6 = f32[2,8,96]{2,1,0:T(8,128)S(1)} copy-done((f32[2,8,96]{2,1,0:T(8,128)S(1)}, f32[2,8,96]{2,1,0:T(8,128)}, u32[]{:S(2)}) %copy-start.6) | copy-done | bytes 6168
  7.5 0.0 copy-start.7
  7.5 0.7 %copy-done.7 = f32[2,8,96]{2,1,0:T(8,128)S(1)} copy-done((f32[2,8,96]{2,1,0:T(8,128)S(1)}, f32[2,8,96]{2,1,0:T(8,128)}, u32[]{:S(2)}) %copy-start.7) | copy-done | bytes 6168
  8.2 39.0 %fused_filter.1 = (bf16[2,64,768]{2,1,0:T(8,128)(2,1)S(1)}, bf16[2,8,96,96]{3,2,1,0:T(8,128)(2,1)S(1)}, bf16[2,8,96,96]{3,2,1,0:T(8,128)(2,1)S(1)}, f32[4,8,96]{2,1,0:T(8,128)S(1)}) custom-call(bf16[16,8,768]{2,1,0:T(8,128)(2,1)S(1)} %bitcast.8, bf16[2,8,8,768]{3,2,1,0:T(8,128)(2,1)S(1)} %bitcast.9, bf16[2,8,96,96]{3,2,1,0:T(8,128)(2,1)S(1)} %copy-done.1, ...), custom_call_target="tpu_custom_call" | custom-call | tf_op jit(solution)/shard_map/fused_filter/pallas_call | solution.py:520
  47.2 0.6 %fusion = (f32[2,8,96]{2,1,0:T(8,128)}, f32[2,8,96]{2,1,0:T(8,128)}) fusion(f32[4,8,96]{2,1,0:T(8,128)S(1)} %get-tuple-element.11), kind=kLoop, calls=%fused_computation.1 | loop fusion | bytes 24576 | tf_op jit(solution)/shard_map/slice | solution.py:568
  47.8 1.0 %convert_element_type.7 = f32[2,8,96,96]{3,2,1,0:T(8,128)} convert(bf16[2,8,96,96]{3,2,1,0:T(8,128)(2,1)S(1)} %get-tuple-element.10) | non-fusion elementwise | flops 147456 | bytes 884736 | tf_op jit(solution)/shard_map/convert_element_type | solution.py:565
  48.8 1.0 %convert_element_type.8 = f32[2,8,96,96]{3,2,1,0:T(8,128)} convert(bf16[2,8,96,96]{3,2,1,0:T(8,128)(2,1)S(1)} %get-tuple-element.12) | non-fusion elementwise | flops 147456 | bytes 884736 | tf_op jit(solution)/shard_map/convert_element_type | solution.py:567
  49.8 0.8 %bitcast_convert_fusion = f32[2,1,8,8,768]{4,3,2,1,0:T(8,128)} fusion(bf16[2,64,768]{2,1,0:T(8,128)(2,1)S(1)} %get-tuple-element.9), kind=kLoop, calls=%fused_computation | loop fusion | flops 98304 | bytes 589824
Async XLA Ops:
  0.6 1.6 %copy-start = (bf16[2,2,512,512]{3,2,1,0:T(8,128)(2,1)S(1)}, bf16[2,2,512,512]{3,2,1,0:T(8,128)(2,1)}, u32[]{:S(2)}) copy-start(bf16[2,2,512,512]{3,2,1,0:T(8,128)(2,1)} %constant.5.clone.refs_7_) | copy-start | bytes 6291460
  2.2 1.0 %copy-start.1 = (bf16[2,8,96,96]{3,2,1,0:T(8,128)(2,1)S(1)}, bf16[2,8,96,96]{3,2,1,0:T(8,128)(2,1)}, u32[]{:S(2)}) copy-start(bf16[2,8,96,96]{3,2,1,0:T(8,128)(2,1)} %refs_2_.1) | copy-start | bytes 884740
  3.2 1.0 %copy-start.2 = (bf16[2,8,96,96]{3,2,1,0:T(8,128)(2,1)S(1)}, bf16[2,8,96,96]{3,2,1,0:T(8,128)(2,1)}, u32[]{:S(2)}) copy-start(bf16[2,8,96,96]{3,2,1,0:T(8,128)(2,1)} %refs_4_.1) | copy-start | bytes 884740
  4.2 0.9 %copy-start.3 = (bf16[1,16,8,768]{3,2,1,0:T(8,128)(2,1)S(1)}, bf16[1,16,8,768]{3,2,1,0:T(8,128)(2,1)}, u32[]{:S(2)}) copy-start(bf16[1,16,8,768]{3,2,1,0:T(8,128)(2,1)} %param.8) | copy-start | bytes 589828
  5.1 0.9 %copy-start.4 = (bf16[2,1,8,8,768]{4,3,2,1,0:T(8,128)(2,1)S(1)}, bf16[2,1,8,8,768]{4,3,2,1,0:T(8,128)(2,1)}, u32[]{:S(2)}) copy-start(bf16[2,1,8,8,768]{4,3,2,1,0:T(8,128)(2,1)} %param.9) | copy-start | bytes 589828
  6.1 0.8 %copy-start.5 = (bf16[2,64,64]{2,1,0:T(8,128)(2,1)S(1)}, bf16[2,64,64]{2,1,0:T(8,128)(2,1)}, u32[]{:S(2)}) copy-start(bf16[2,64,64]{2,1,0:T(8,128)(2,1)} %constant.4.clone.refs_6_) | copy-start | bytes 49156
  6.8 0.7 %copy-start.6 = (f32[2,8,96]{2,1,0:T(8,128)S(1)}, f32[2,8,96]{2,1,0:T(8,128)}, u32[]{:S(2)}) copy-start(f32[2,8,96]{2,1,0:T(8,128)} %refs_3_.1) | copy-start | bytes 18436
  7.5 0.7 %copy-start.7 = (f32[2,8,96]{2,1,0:T(8,128)S(1)}, f32[2,8,96]{2,1,0:T(8,128)}, u32[]{:S(2)}) copy-start(f32[2,8,96]{2,1,0:T(8,128)} %refs_5_.1) | copy-start | bytes 18436

commit v2 on v1

--- a/solution.py
+++ b/solution.py
@@ -176,8 +176,13 @@
 def row_tables(height, inner):
     cosine, sine = phase_tables(height, height)
     eye = np.eye(inner)
-    both = np.stack([np.kron(cosine.T, eye), np.kron(sine.T, eye)])
-    return split_table(both)
+    both = np.stack([cosine.T, sine.T])
+    scales = np.linspace(1.0, 2.0, 2001)
+    errors = [
+        np.mean(((both * a).astype(jnp.bfloat16).astype(np.float64) / a - both) ** 2) for a in scales
+    ]
+    scale = float(scales[int(np.argmin(errors))])
+    return np.stack([np.kron(part * scale, eye) for part in both]).astype(jnp.bfloat16), 1.0 / scale
 
 
 def padded(values, lanes):
@@ -185,20 +190,59 @@
     return jnp.concatenate([values, jnp.zeros((rows, lanes - columns), values.dtype)], axis=1)
 
 
+def fold(matrix, bias, lanes):
+    width = matrix.shape[0]
+    side = lanes - width
+    keep = width * width // lanes
+    rest = matrix[keep:]
+    tail = jnp.concatenate(
+        [rest[:, t * side : (t + 1) * side] for t in range(width // side)], axis=0
+    )
+    top = jnp.concatenate([matrix[:keep], tail], axis=1)
+    return jnp.concatenate([top, bias], axis=0)
+
+
+def unpack_kernel(gather_ref, arrived_ref, filt_ref, inner_ref, inner_off_ref, outer_ref, outer_off_ref):
+    blocks = arrived_ref.shape[0]
+    width = inner_ref.shape[2]
+    lanes = gather_ref.shape[-1]
+    side = lanes - width
+    keep = width * width // lanes
+    step = width - keep
+    f32 = jnp.float32
+    m_local = filt_ref.shape[1]
+    k_local = filt_ref.shape[2]
+    for p in range(2):
+        whole = jnp.concatenate(
+            [arrived_ref[b, :, p * lanes : p * lanes + width].astype(f32) for b in range(blocks)],
+            axis=1,
+        )
+        for m in range(m_local):
+            filt_ref[p, m] = whole[m * k_local : (m + 1) * k_local]
+    for q in range(4):
+        grad = inner_ref if q < 2 else outer_ref
+        off = inner_off_ref if q < 2 else outer_off_ref
+        for b in range(blocks):
+            piece = gather_ref[b % 2, q, b // 2].astype(f32)
+            grad[q % 2, b, 0:keep, :] = piece[0:keep, 0:width]
+            grad[q % 2, b, keep:width, :] = jnp.concatenate(
+                [piece[t * step : (t + 1) * step, width:lanes] for t in range(width // side)], axis=1
+            )
+            off[q % 2, b : b + 1, :] = piece[keep : keep + 1, 0:width]
+
+
 def fused_kernel(
     sizes,
-    fields_ref,
-    cot_ref,
+    fields_hbm,
+    cot_hbm,
     inner_ref,
-    inner_off_ref,
+    inner_off_hbm,
     outer_ref,
-    outer_off_ref,
-    cols_ref,
+    outer_off_hbm,
+    cols_hbm,
     rows_hbm,
-    filt_ref,
-    inner_grad_ref,
-    outer_grad_ref,
-    bias_ref,
+    gather,
+    recv_d,
     send_a,
     recv_a,
     send_b,
@@ -206,10 +250,8 @@
     send_c,
     recv_c,
     send_d,
-    recv_d,
     send_e,
     recv_e,
-    gather,
     spec_s,
     hid_s,
     back_s,
@@ -218,58 +260,76 @@
     w1,
     w2,
     rows_ref,
+    cols_ref,
+    fields_ref,
+    cot_ref,
+    inner_off_ref,
+    outer_off_ref,
     lon_send,
     lon_recv,
     lat_send,
     lat_recv,
+    z_send,
+    z_recv,
+    spread_send,
+    spread_recv,
     core_send,
     core_recv,
     local_sem,
 ):
-    lats, lons, blocks, width, lanes, normalizer = sizes
+    lats, lons, blocks, width, lanes, normalizer, unscale = sizes
     i = lax.axis_index("lat")
     j = lax.axis_index("lon")
-    h_local, w_local, _ = fields_ref.shape
+    h_local = fields_ref.shape[0]
     m_local, k_local = cot_ref.shape[1], cot_ref.shape[2]
     tokens = spec_s.shape[0]
     part_rows = m_local * k_local
     zs = lons // 2
     f32, bf16 = jnp.float32, jnp.bfloat16
-
-    loads = [pltpu.make_async_copy(rows_hbm, rows_ref, local_sem.at[0])]
-    for p in range(2):
-        loads.append(
-            pltpu.make_async_copy(inner_ref.at[p, j], raw_w.at[p], local_sem.at[1 + p])
-        )
-        loads.append(
-            pltpu.make_async_copy(outer_ref.at[p, j], raw_w.at[2 + p], local_sem.at[3 + p])
-        )
-    for load in loads:
-        load.start()
+    mesh_id = pl.DeviceIdType.MESH
 
     barrier = pltpu.get_barrier_semaphore()
 
     def greet_lon(d, carry):
         pl.semaphore_signal(
-            barrier, inc=1, device_id=(i, lax.rem(j + d, lons)), device_id_type=pl.DeviceIdType.MESH
+            barrier, inc=1, device_id=(i, lax.rem(j + d, lons)), device_id_type=mesh_id
         )
         return carry
 
     def greet_lat(d, carry):
         pl.semaphore_signal(
-            barrier, inc=1, device_id=(lax.rem(i + d, lats), j), device_id_type=pl.DeviceIdType.MESH
+            barrier, inc=1, device_id=(lax.rem(i + d, lats), j), device_id_type=mesh_id
         )
         return carry
 
+    sources = [
+        (fields_hbm, fields_ref),
+        (cot_hbm, cot_ref),
+        (cols_hbm, cols_ref),
+        (inner_off_hbm, inner_off_ref),
+        (outer_off_hbm, outer_off_ref),
+        (inner_ref.at[0, j], raw_w.at[0]),
+        (inner_ref.at[1, j], raw_w.at[1]),
+        (outer_ref.at[0, j], raw_w.at[2]),
+        (outer_ref.at[1, j], raw_w.at[3]),
+        (rows_hbm, rows_ref),
+    ]
+    loads = [
+        pltpu.make_async_copy(source, target, local_sem.at[n])
+        for n, (source, target) in enumerate(sources)
+    ]
+    loads[0].start()
     lax.fori_loop(1, lons, greet_lon, 0)
     lax.fori_loop(1, lats, greet_lat, 0)
-
-    for h in range(h_local):
-        row = fields_ref[h].astype(f32)
-        for b in range(blocks):
-            send_a[b, :, h * lanes : (h + 1) * lanes] = padded(
-                row[:, b * width : (b + 1) * width], lanes
-            ).astype(bf16)
+    for load in loads[1:]:
+        load.start()
+    loads[0].wait()
+
+    rows_of = [fields_ref[h].astype(f32) for h in range(h_local)]
+    for b in range(blocks):
+        send_a[b] = jnp.concatenate(
+            [row[:, b * width : (b + 1) * width] for row in rows_of], axis=1
+        ).astype(bf16)
 
     pl.semaphore_wait(barrier, lons + lats - 2)
 
@@ -280,7 +340,7 @@
             send_sem=lon_send.at[phase, d],
             recv_sem=lon_recv.at[phase, d],
             device_id=(i, lax.rem(j + d, lons)),
-            device_id_type=pl.DeviceIdType.MESH,
+            device_id_type=mesh_id,
         )
 
     def lat_copy(phase, src, dst, d):
@@ -290,7 +350,7 @@
             send_sem=lat_send.at[phase, d],
             recv_sem=lat_recv.at[phase, d],
             device_id=(lax.rem(i + d, lats), j),
-            device_id_type=pl.DeviceIdType.MESH,
+            device_id_type=mesh_id,
         )
 
     def exchange_start(copy, phase, send, recv, me, n):
@@ -318,6 +378,7 @@
     exchange_start(lon_copy, 0, send_a, recv_a, j, lons)
     recv_a[j] = send_a[j]
 
+    loads[1].wait()
     for p in range(2):
         part = jnp.concatenate([cot_ref[p, m].astype(f32) for m in range(m_local)], axis=0)
         for b in range(blocks):
@@ -327,7 +388,7 @@
     exchange_start(lon_copy, 1, send_c, recv_c, j, lons)
     recv_c[j] = send_c[j]
 
-    for load in loads[1:]:
+    for load in loads[2:]:
         load.wait()
     w1[...] = jnp.zeros_like(w1)
     w2[...] = jnp.zeros_like(w2)
@@ -343,7 +404,6 @@
     off2 = jnp.concatenate(
         [padded(outer_off_ref[p, pl.ds(j, 1), :], lanes) for p in range(2)], axis=1
     )
-    loads[0].wait()
 
     exchange_recv(lon_copy, 0, send_a, recv_a, j, lons)
     columns = jnp.concatenate([recv_a[s].astype(f32) for s in range(lons)], axis=0).astype(bf16)
@@ -351,15 +411,20 @@
         cols_ref[1], columns, preferred_element_type=f32
     )
     for g in range(lats):
+        high, low = [], []
         for p in range(2):
             first = (2 * g + p) * k_local
-            send_b[g, :, p * lanes : (p + 1) * lanes] = jnp.concatenate(
+            value = jnp.concatenate(
                 [
-                    half[first : first + k_local, h * lanes : (h + 1) * lanes]
+                    half[first : first + k_local, h * width : (h + 1) * width]
                     for h in range(h_local)
                 ],
                 axis=0,
-            ).astype(bf16)
+            )
+            top = value.astype(bf16).astype(f32)
+            high.append(top)
+            low.append(value - top)
+        send_b[g] = jnp.concatenate(high + low, axis=1).astype(bf16)
     exchange_start(lat_copy, 0, send_b, recv_b, i, lats)
     recv_b[i] = send_b[i]
     exchange_recv(lon_copy, 1, send_c, recv_c, j, lons)
@@ -368,22 +433,21 @@
     chunks = 4
     chunk = tokens // chunks
     per_chunk = lons // chunks
-    lane = lax.broadcasted_iota(jnp.int32, (chunk, 2 * lanes), 1)
-    ones_lane = lane == width
+    packed = jnp.concatenate([recv_b[s].astype(f32) for s in range(lats)], axis=0)
+    lines = jnp.concatenate(
+        [padded(packed[:, t * width : (t + 1) * width], lanes) for t in range(4)], axis=1
+    ).astype(bf16)
+    ones_lane = lax.broadcasted_iota(jnp.int32, (chunk, 2 * lanes), 1) == width
     one = jnp.ones((chunk, 2 * lanes), f32)
-
-    def block_layers(c, carry):
-        rows = pl.ds(pl.multiple_of(c * chunk, chunk), chunk)
-        lines = recv_b[...].reshape(tokens, 2 * lanes)
-        cos_part = jnp.dot(rows_ref[0, 0, rows, :], lines, preferred_element_type=f32) + jnp.dot(
-            rows_ref[1, 0, rows, :], lines, preferred_element_type=f32
-        )
-        sin_part = jnp.dot(rows_ref[0, 1, rows, :], lines, preferred_element_type=f32) + jnp.dot(
-            rows_ref[1, 1, rows, :], lines, preferred_element_type=f32
-        )
+    for c in range(chunks):
+        rows = slice(c * chunk, (c + 1) * chunk)
+        cos_part = jnp.dot(rows_ref[0, rows, :], lines, preferred_element_type=f32)
+        sin_part = jnp.dot(rows_ref[1, rows, :], lines, preferred_element_type=f32)
+        cos_part = cos_part[:, : 2 * lanes] + cos_part[:, 2 * lanes :]
+        sin_part = sin_part[:, : 2 * lanes] + sin_part[:, 2 * lanes :]
         real = cos_part[:, :lanes] + sin_part[:, lanes:]
         imag = cos_part[:, lanes:] - sin_part[:, :lanes]
-        spec_wide = jnp.concatenate([real, imag], axis=1)
+        spec_wide = jnp.concatenate([real, imag], axis=1) * unscale
         spec = spec_wide.astype(bf16)
         spec_s[rows, :] = jnp.where(ones_lane, one, spec_wide).astype(bf16)
         pre = jnp.dot(spec, w1[...], preferred_element_type=f32) + off1
@@ -397,29 +461,37 @@
         out = jnp.dot(hid_wide.astype(bf16), w2[...], preferred_element_type=f32) + off2
         soft = jnp.tanh(out * (1.0 / shrink_level))
         filtered = (out - shrink_level * soft).astype(bf16)
-        send_d[pl.ds(c * per_chunk, per_chunk)] = filtered.reshape(
-            per_chunk, part_rows, 2 * lanes
-        )
-        cot = recv_c[pl.ds(c * per_chunk, per_chunk)].reshape(chunk, 2 * lanes).astype(f32)
+        for r in range(per_chunk):
+            dest = c * per_chunk + r
+            send_d[dest] = filtered[r * part_rows : (r + 1) * part_rows]
+
+            @pl.when(dest != j)
+            def _():
+                away = lax.rem(dest - j + lons, lons)
+                lon_copy(2, send_d.at[dest], recv_d.at[j], away).start()
+
+        cot = jnp.concatenate(
+            [recv_c[c * per_chunk + r] for r in range(per_chunk)], axis=0
+        ).astype(f32)
         back = (cot * (soft * soft)).astype(bf16)
         back_s[rows, :] = back
         turned = lax.dot_general(
             back, w2[...], (((1,), (1,)), ((), ())), preferred_element_type=f32
         )
         hb_s[rows, :] = (turned * slope).astype(bf16)
-        return carry
-
-    lax.fori_loop(0, chunks, block_layers, 0)
-    exchange_start(lon_copy, 2, send_d, recv_d, j, lons)
     recv_d[j] = send_d[j]
 
-    deep = send_e.shape[1]
+    extra = send_e.shape[1] - width * width // lanes
     for base, left, right in ((2, hid_s, back_s), (0, spec_s, hb_s)):
         full = lax.dot_general(
             left[...], right[...], (((0,), (0,)), ((), ())), preferred_element_type=f32
         )
-        send_e[base] = (full[0:deep, :lanes] + full[lanes : lanes + deep, lanes:]).astype(bf16)
-        send_e[base + 1] = (full[0:deep, lanes:] - full[lanes : lanes + deep, :lanes]).astype(bf16)
+        first = full[:lanes, :lanes] + full[lanes:, lanes:]
+        second = full[:lanes, lanes:] - full[lanes:, :lanes]
+        for n, value in enumerate((first, second)):
+            send_e[base + n] = fold(
+                value[:width, :width], value[width : width + extra], lanes
+            ).astype(bf16)
     exchange_start(lat_copy, 1, send_e, recv_e, i, lats)
     recv_e[i] = send_e[i]
     exchange_recv(lat_copy, 1, send_e, recv_e, i, lats)
@@ -434,10 +506,20 @@
         return pltpu.make_async_remote_copy(
             src_ref=gather.at[side, i, slot],
             dst_ref=gather.at[side, i, slot],
-            send_sem=lon_send.at[3, d],
-            recv_sem=lon_recv.at[3, d],
+            send_sem=z_send.at[d],
+            recv_sem=z_recv.at[d],
             device_id=(i, lax.rem(j + 2 * d, lons)),
-            device_id_type=pl.DeviceIdType.MESH,
+            device_id_type=mesh_id,
+        )
+
+    def spread_copy(d, row, slot, turn):
+        return pltpu.make_async_remote_copy(
+            src_ref=gather.at[side, row, slot],
+            dst_ref=gather.at[side, row, slot],
+            send_sem=spread_send.at[turn, d],
+            recv_sem=spread_recv.at[turn, d],
+            device_id=(lax.rem(i + d, lats), j),
+            device_id_type=mesh_id,
         )
 
     def side_copy(from_side, slot):
@@ -447,39 +529,25 @@
             send_sem=core_send.at[slot],
             recv_sem=core_recv.at[slot],
             device_id=(i, j + 1 - 2 * side),
-            device_id_type=pl.DeviceIdType.MESH,
+            device_id_type=mesh_id,
         )
 
     for d in range(1, zs):
         z_copy(d, z).start()
-
-    exchange_recv(lon_copy, 2, send_d, recv_d, j, lons)
-    for p in range(2):
-        filt_ref[p] = jnp.concatenate(
-            [recv_d[b, :, p * lanes : p * lanes + width].astype(f32) for b in range(blocks)],
-            axis=1,
-        ).astype(bf16)
-
-    for d in range(1, zs):
-        z_copy(d, lax.rem(z + zs - d, zs)).wait_recv()
-    for d in range(1, lats):
-        lat_copy(2, gather.at[side, i], gather.at[side, i], d).start()
+    for turn in range(zs):
+        slot = lax.rem(z + zs - turn, zs)
+        if turn:
+            z_copy(turn, slot).wait_recv()
+        for d in range(1, lats):
+            spread_copy(d, i, slot, turn).start()
     side_copy(side, i).start()
     for d in range(1, lats):
         source = lax.rem(i + lats - d, lats)
-        lat_copy(2, gather.at[side, source], gather.at[side, source], d).wait_recv()
+        for turn in range(zs):
+            spread_copy(d, source, lax.rem(z + zs - turn, zs), turn).wait_recv()
         side_copy(side, source).start()
-    other = 1 - side
-    for q in range(lats):
-        side_copy(other, q).wait_recv()
-
-    for q in range(lats):
-        target = inner_grad_ref if q < 2 else outer_grad_ref
-        for b in range(blocks):
-            piece = gather[b % 2, q, b // 2]
-            target[q % 2, b] = piece[0:width, 0:width]
-            bias_ref[q, b : b + 1, :] = piece[width:deep, 0:width].astype(f32)[0:1]
-
+
+    exchange_recv(lon_copy, 2, send_d, recv_d, j, lons)
     exchange_sent(lon_copy, 0, send_a, recv_a, j, lons)
     exchange_sent(lon_copy, 1, send_c, recv_c, j, lons)
     exchange_sent(lon_copy, 2, send_d, recv_d, j, lons)
@@ -487,10 +555,13 @@
     exchange_sent(lat_copy, 1, send_e, recv_e, i, lats)
     for d in range(1, zs):
         z_copy(d, z).wait_send()
-    for d in range(1, lats):
-        lat_copy(2, gather.at[side, i], gather.at[side, i], d).wait_send()
+    for turn in range(zs):
+        for d in range(1, lats):
+            spread_copy(d, i, lax.rem(z + zs - turn, zs), turn).wait_send()
     for q in range(lats):
         side_copy(side, q).wait_send()
+    for q in range(lats):
+        side_copy(1 - side, q).wait_recv()
 
 
 def fused_device(fields, spec_cotangent, inner_kernel, inner_offset, outer_kernel, outer_offset):
@@ -504,51 +575,60 @@
     lanes = 128
     tokens = height * k_local
     part_rows = m_local * k_local
-    deep = (width // 16 + 1) * 16
+    deep = width * width // lanes + 8
     normalizer = 1.0 / math.sqrt(height * wavenumbers)
     cols = jnp.asarray(column_tables(full_width, wavenumbers, lats))
-    rows = jnp.asarray(row_tables(height, k_local))
+    rows, unscale = row_tables(height, k_local)
+    rows = jnp.asarray(rows)
     vmem = pl.BlockSpec(memory_space=pltpu.VMEM)
-    hbm = pl.BlockSpec(memory_space=pl.ANY)
-    bf16 = jnp.bfloat16
+    hbm = pl.BlockSpec(memory_space=pltpu.HBM)
+    bf16, f32 = jnp.bfloat16, jnp.float32
     wide = (tokens, 2 * lanes)
     dma = pltpu.SemaphoreType.DMA
 
     def pair(*shape):
         return [pltpu.VMEM(shape, bf16)] * 2
 
-    filt, inner_grad, outer_grad, bias = pl.pallas_call(
-        lambda *refs: fused_kernel((lats, lons, blocks, width, lanes, normalizer), *refs),
+    gathered, arrived = pl.pallas_call(
+        lambda *refs: fused_kernel(
+            (lats, lons, blocks, width, lanes, normalizer, unscale), *refs
+        ),
         name="fused_filter",
         out_shape=[
-            jax.ShapeDtypeStruct((2, part_rows, channels), bf16),
-            jax.ShapeDtypeStruct(inner_kernel.shape, bf16),
-            jax.ShapeDtypeStruct(outer_kernel.shape, bf16),
-            jax.ShapeDtypeStruct((4, blocks, width), jnp.float32),
+            jax.ShapeDtypeStruct((2, lats, lons // 2, deep, lanes), bf16),
+            jax.ShapeDtypeStruct((blocks, part_rows, 2 * lanes), bf16),
         ],
-        in_specs=[vmem, vmem, hbm, vmem, hbm, vmem, vmem, hbm],
-        out_specs=[vmem] * 4,
+        in_specs=[hbm] * 8,
+        out_specs=[vmem] * 2,
         scratch_shapes=[
-            *pair(blocks, w_local, h_local * lanes),
-            *pair(lats, h_local * k_local, 2 * lanes),
+            *pair(blocks, w_local, h_local * width),
+            *pair(lats, h_local * k_local, 4 * width),
             *pair(blocks, part_rows, 2 * lanes),
-            *pair(blocks, part_rows, 2 * lanes),
+            pltpu.VMEM((blocks, part_rows, 2 * lanes), bf16),
             *pair(4, deep, lanes),
-            pltpu.VMEM((2, lats, lons // 2, deep, lanes), bf16),
             *[pltpu.VMEM(wide, bf16)] * 4,
             pltpu.VMEM((4, width, width), bf16),
             *pair(2 * lanes, 2 * lanes),
             pltpu.VMEM(rows.shape, bf16),
-            dma((4, lons)),
-            dma((4, lons)),
-            dma((3, lats)),
-            dma((3, lats)),
+            pltpu.VMEM(cols.shape, bf16),
+            pltpu.VMEM(fields.shape[1:], bf16),
+            pltpu.VMEM((2, m_local, k_local, channels), bf16),
+            pltpu.VMEM(inner_offset.shape, f32),
+            pltpu.VMEM(outer_offset.shape, f32),
+            dma((3, lons)),
+            dma((3, lons)),
+            dma((2, lats)),
+            dma((2, lats)),
+            dma((lons // 2,)),
+            dma((lons // 2,)),
+            dma((lons // 2, lats)),
+            dma((lons // 2, lats)),
             dma((lats,)),
             dma((lats,)),
-            dma((5,)),
+            dma((10,)),
         ],
         compiler_params=pltpu.CompilerParams(
-            collective_id=0, has_side_effects=True, vmem_limit_bytes=40 * 1024 * 1024
+            collective_id=0, has_side_effects=True, vmem_limit_bytes=63 * 1024 * 1024
         ),
     )(
         fields.reshape(fields.shape[1:]),
@@ -560,12 +640,25 @@
         cols,
         rows,
     )
+    filt, inner_grad, inner_bias, outer_grad, outer_bias = pl.pallas_call(
+        unpack_kernel,
+        name="unpack",
+        out_shape=[
+            jax.ShapeDtypeStruct((2, m_local, k_local, channels), f32),
+            jax.ShapeDtypeStruct(inner_kernel.shape, f32),
+            jax.ShapeDtypeStruct(inner_offset.shape, f32),
+            jax.ShapeDtypeStruct(outer_kernel.shape, f32),
+            jax.ShapeDtypeStruct(outer_offset.shape, f32),
+        ],
+        in_specs=[vmem] * 2,
+        out_specs=[vmem] * 5,
+    )(gathered, arrived)
     return (
-        filt.astype(jnp.float32).reshape(spec_cotangent.shape),
-        inner_grad.astype(jnp.float32),
-        bias[0:2],
-        outer_grad.astype(jnp.float32),
-        bias[2:4],
+        filt.reshape(spec_cotangent.shape),
+        inner_grad,
+        inner_bias,
+        outer_grad,
+        outer_bias,
     )
 
 
@@ -576,8 +669,7 @@
         fields.shape[0] == 1
         and lons == blocks
         and lats == 4
-        and width % 16 == 0
-        and width < 128
+        and width == 96
         and fields.shape[1] == 16
         and fields.shape[2] == 8
         and spec_cotangent.shape[2] == 8

time: 51.3 us -> 40.3 us (0.79)
  local copies, waits for them, and re-layouts: 8.19 us -> 0 us
  other arithmetic: 2.69 us -> 0 us
    unnamed x16 -> x0, local copies, waits for them, and re-layouts: 7.58 us -> none
    pallas_call x0 -> x1, Pallas kernels: none -> 2.63 us  [fused_device(): pl.pallas_call(unpack_kernel, name='unpack', out_shape=[jax.ShapeDtypeStr...]
    pallas_call x1, Pallas kernels: 39 us -> 36.4 us  [fused_device(): pl.pallas_call(lambda *refs: fused_kernel((lats, lons, blocks, width, lan...]
    convert_element_type x2 -> x0, other arithmetic: 1.91 us -> none  [the longest x1 0.96 us: fused_device(): inner_grad.astype(jnp.float32)]
    unnamed x1 -> x0, other arithmetic: 0.77 us -> none
    slice x1 -> x0, local copies, waits for them, and re-layouts: 0.61 us -> none  [fused_device(): bias[2:4]]
where the time goes in v2:
time: 40.3 us; the launch traced here: 39.7 us
  Pallas kernels  39 us (97%)
  between operations  0.64 us (2%)
    pallas_call x1, Pallas kernels, fused_device(): pl.pallas_call(lambda *refs: fused_kernel((lats, lons, blocks, width, lan...  36.4 us
    pallas_call x1, Pallas kernels, fused_device(): pl.pallas_call(unpack_kernel, name='unpack', out_shape=[jax.ShapeDtypeStr...  2.63 us

profile of v2, /device:TPU:0, one launch (start us, length us, event | category | flops | bytes accessed | tf_op | source)
XLA Modules:
  0.0 39.7 jit_solution(292264645384674192)
XLA Ops:
  0.6 36.4 %fused_filter.1 = (bf16[2,4,4,80,128]{4,3,2,1,0:T(8,128)(2,1)}, bf16[8,64,256]{2,1,0:T(8,128)(2,1)}) custom-call(bf16[16,8,768]{2,1,0:T(8,128)(2,1)} %bitcast.5, bf16[2,8,8,768]{3,2,1,0:T(8,128)(2,1)} %bitcast.6, bf16[2,8,96,96]{3,2,1,0:T(8,128)(2,1)} %refs_2_.1, f32[2,8,96]{2,1,0:T(8,128)} %refs_3_.1, bf16[2,8,96,96]{3,2,1,0:T(8,128)(2,1)} %refs_4_.1, ...), custom_call_target="tpu_custom_call" | custom-call | tf_op jit(solution)/shard_map/fused_filter/pallas_call | solution.py:592
  37.0 2.6 %unpack.1 = (f32[2,8,8,768]{3,2,1,0:T(8,128)}, f32[2,8,96,96]{3,2,1,0:T(8,128)}, f32[2,8,96]{2,1,0:T(8,128)}, f32[2,8,96,96]{3,2,1,0:T(8,128)}, f32[2,8,96]{2,1,0:T(8,128)}) custom-call(bf16[2,4,4,80,128]{4,3,2,1,0:T(8,128)(2,1)} %get-tuple-element.12.gather_ref, bf16[8,64,256]{2,1,0:T(8,128)(2,1)} %get-tuple-element.13.arrived_ref), custom_call_target="tpu_custom_call" | custom-call | tf_op jit(solution)/shard_map/unpack/pallas_call | solution.py:643

commit v3 on v2

--- a/solution.py
+++ b/solution.py
@@ -202,33 +202,75 @@
     return jnp.concatenate([top, bias], axis=0)
 
 
-def unpack_kernel(gather_ref, arrived_ref, filt_ref, inner_ref, inner_off_ref, outer_ref, outer_off_ref):
+def two_halves(pair, width, lanes):
+    rows = pair.shape[0] // 2
+    return jnp.concatenate(
+        [
+            pair[half * rows : (half + 1) * rows, p * lanes : p * lanes + width]
+            for half in range(2)
+            for p in range(2)
+        ],
+        axis=1,
+    )
+
+
+def unpack_kernel(
+    gather_hbm,
+    arrived_hbm,
+    filt_hbm,
+    inner_hbm,
+    inner_off_hbm,
+    outer_hbm,
+    outer_off_hbm,
+    gather_ref,
+    arrived_ref,
+    filt_ref,
+    grad_ref,
+    off_ref,
+    sems,
+):
     blocks = arrived_ref.shape[0]
-    width = inner_ref.shape[2]
+    width = grad_ref.shape[2]
     lanes = gather_ref.shape[-1]
     side = lanes - width
     keep = width * width // lanes
     step = width - keep
     f32 = jnp.float32
-    m_local = filt_ref.shape[1]
-    k_local = filt_ref.shape[2]
+    m_local, k_local = filt_ref.shape[1:3]
+    loads = [
+        pltpu.make_async_copy(arrived_hbm, arrived_ref, sems.at[0]),
+        pltpu.make_async_copy(gather_hbm, gather_ref, sems.at[1]),
+    ]
+    for load in loads:
+        load.start()
+    stores = []
+    loads[0].wait()
+    groups = [arrived_ref[b].astype(f32) for b in range(blocks)]
     for p in range(2):
-        whole = jnp.concatenate(
-            [arrived_ref[b, :, p * lanes : p * lanes + width].astype(f32) for b in range(blocks)],
-            axis=1,
-        )
-        for m in range(m_local):
-            filt_ref[p, m] = whole[m * k_local : (m + 1) * k_local]
+        for half in range(2):
+            first = (2 * half + p) * width
+            whole = jnp.concatenate([group[:, first : first + width] for group in groups], axis=1)
+            for m in range(m_local // 2):
+                filt_ref[p, half * (m_local // 2) + m] = whole[m * k_local : (m + 1) * k_local]
+        stores.append(pltpu.make_async_copy(filt_ref.at[p], filt_hbm.at[p], sems.at[2 + p]))
+        stores[-1].start()
+    loads[1].wait()
     for q in range(4):
-        grad = inner_ref if q < 2 else outer_ref
-        off = inner_off_ref if q < 2 else outer_off_ref
         for b in range(blocks):
             piece = gather_ref[b % 2, q, b // 2].astype(f32)
-            grad[q % 2, b, 0:keep, :] = piece[0:keep, 0:width]
-            grad[q % 2, b, keep:width, :] = jnp.concatenate(
+            grad_ref[q, b, 0:keep, :] = piece[0:keep, 0:width]
+            grad_ref[q, b, keep:width, :] = jnp.concatenate(
                 [piece[t * step : (t + 1) * step, width:lanes] for t in range(width // side)], axis=1
             )
-            off[q % 2, b : b + 1, :] = piece[keep : keep + 1, 0:width]
+            off_ref[q, b : b + 1, :] = piece[keep : keep + 1, 0:width]
+        grad = inner_hbm if q < 2 else outer_hbm
+        off = inner_off_hbm if q < 2 else outer_off_hbm
+        stores.append(pltpu.make_async_copy(grad_ref.at[q], grad.at[q % 2], sems.at[4 + q]))
+        stores.append(pltpu.make_async_copy(off_ref.at[q], off.at[q % 2], sems.at[8 + q]))
+        stores[-2].start()
+        stores[-1].start()
+    for store in stores:
+        store.wait()
 
 
 def fused_kernel(
@@ -379,13 +421,17 @@
     recv_a[j] = send_a[j]
 
     loads[1].wait()
-    for p in range(2):
-        part = jnp.concatenate([cot_ref[p, m].astype(f32) for m in range(m_local)], axis=0)
-        for b in range(blocks):
-            send_c[b, :, p * lanes : (p + 1) * lanes] = padded(
-                part[:, b * width : (b + 1) * width], lanes
-            ).astype(bf16)
-    exchange_start(lon_copy, 1, send_c, recv_c, j, lons)
+    quarters = [
+        jnp.concatenate(
+            [cot_ref[p, half * (m_local // 2) + m].astype(f32) for m in range(m_local // 2)], axis=0
+        )
+        for half in range(2)
+        for p in range(2)
+    ]
+    for b in range(blocks):
+        send_c[b] = jnp.concatenate(
+            [part[:, b * width : (b + 1) * width] for part in quarters], axis=1
+        ).astype(bf16)
     recv_c[j] = send_c[j]
 
     for load in loads[2:]:
@@ -406,6 +452,7 @@
     )
 
     exchange_recv(lon_copy, 0, send_a, recv_a, j, lons)
+    exchange_start(lon_copy, 1, send_c, recv_c, j, lons)
     columns = jnp.concatenate([recv_a[s].astype(f32) for s in range(lons)], axis=0).astype(bf16)
     half = jnp.dot(cols_ref[0], columns, preferred_element_type=f32) + jnp.dot(
         cols_ref[1], columns, preferred_element_type=f32
@@ -425,9 +472,12 @@
             high.append(top)
             low.append(value - top)
         send_b[g] = jnp.concatenate(high + low, axis=1).astype(bf16)
-    exchange_start(lat_copy, 0, send_b, recv_b, i, lats)
+
+        @pl.when(g != i)
+        def _():
+            lat_copy(0, send_b.at[g], recv_b.at[i], lax.rem(g - i + lats, lats)).start()
+
     recv_b[i] = send_b[i]
-    exchange_recv(lon_copy, 1, send_c, recv_c, j, lons)
     exchange_recv(lat_copy, 0, send_b, recv_b, i, lats)
 
     chunks = 4
@@ -460,19 +510,27 @@
         hid_s[rows, :] = jnp.where(ones_lane, one, hid_wide).astype(bf16)
         out = jnp.dot(hid_wide.astype(bf16), w2[...], preferred_element_type=f32) + off2
         soft = jnp.tanh(out * (1.0 / shrink_level))
-        filtered = (out - shrink_level * soft).astype(bf16)
+        filtered = out - shrink_level * soft
         for r in range(per_chunk):
             dest = c * per_chunk + r
-            send_d[dest] = filtered[r * part_rows : (r + 1) * part_rows]
+            send_d[dest] = two_halves(
+                filtered[r * part_rows : (r + 1) * part_rows], width, lanes
+            ).astype(bf16)
 
             @pl.when(dest != j)
             def _():
                 away = lax.rem(dest - j + lons, lons)
                 lon_copy(2, send_d.at[dest], recv_d.at[j], away).start()
 
-        cot = jnp.concatenate(
-            [recv_c[c * per_chunk + r] for r in range(per_chunk)], axis=0
-        ).astype(f32)
+        if c == 0:
+            exchange_recv(lon_copy, 1, send_c, recv_c, j, lons)
+        parts = []
+        for r in range(per_chunk):
+            group = recv_c[c * per_chunk + r].astype(f32)
+            fours = [padded(group[:, t * width : (t + 1) * width], lanes) for t in range(4)]
+            parts.append(jnp.concatenate(fours[0:2], axis=1))
+            parts.append(jnp.concatenate(fours[2:4], axis=1))
+        cot = jnp.concatenate(parts, axis=0)
         back = (cot * (soft * soft)).astype(bf16)
         back_s[rows, :] = back
         turned = lax.dot_general(
@@ -596,15 +654,15 @@
         name="fused_filter",
         out_shape=[
             jax.ShapeDtypeStruct((2, lats, lons // 2, deep, lanes), bf16),
-            jax.ShapeDtypeStruct((blocks, part_rows, 2 * lanes), bf16),
+            jax.ShapeDtypeStruct((blocks, part_rows // 2, 4 * width), bf16),
         ],
         in_specs=[hbm] * 8,
         out_specs=[vmem] * 2,
         scratch_shapes=[
             *pair(blocks, w_local, h_local * width),
             *pair(lats, h_local * k_local, 4 * width),
-            *pair(blocks, part_rows, 2 * lanes),
-            pltpu.VMEM((blocks, part_rows, 2 * lanes), bf16),
+            *pair(blocks, part_rows // 2, 4 * width),
+            pltpu.VMEM((blocks, part_rows // 2, 4 * width), bf16),
             *pair(4, deep, lanes),
             *[pltpu.VMEM(wide, bf16)] * 4,
             pltpu.VMEM((4, width, width), bf16),
@@ -650,8 +708,17 @@
             jax.ShapeDtypeStruct(outer_kernel.shape, f32),
             jax.ShapeDtypeStruct(outer_offset.shape, f32),
         ],
-        in_specs=[vmem] * 2,
-        out_specs=[vmem] * 5,
+        in_specs=[hbm] * 2,
+        out_specs=[hbm] * 5,
+        scratch_shapes=[
+            pltpu.VMEM(gathered.shape, bf16),
+            pltpu.VMEM(arrived.shape, bf16),
+            pltpu.VMEM((2, m_local, k_local, channels), f32),
+            pltpu.VMEM((4, blocks, width, width), f32),
+            pltpu.VMEM((4, blocks, width), f32),
+            dma((12,)),
+        ],
+        compiler_params=pltpu.CompilerParams(vmem_limit_bytes=63 * 1024 * 1024),
     )(gathered, arrived)
     return (
         filt.reshape(spec_cotangent.shape),

time: 40.3 us -> 39.6 us (0.983); the launches traced: 39.7 us -> 39.5 us
  no operation moved by 1% of the time
where the time goes in v3:
time: 39.6 us; the launch traced here: 39.5 us
  Pallas kernels  38.8 us (98%)
  between operations  0.64 us (2%)
    pallas_call x1, Pallas kernels, fused_device(): pl.pallas_call(lambda *refs: fused_kernel((lats, lons, blocks, width, lan...  36.3 us
    pallas_call x1, Pallas kernels, fused_device(): pl.pallas_call(unpack_kernel, name='unpack', out_shape=[jax.ShapeDtypeStr...  2.56 us

profile of v3, /device:TPU:0, one launch (start us, length us, event | category | flops | bytes accessed | tf_op | source)
XLA Modules:
  0.0 39.5 jit_solution(16942572644554284341)
XLA Ops:
  0.6 36.3 %fused_filter.1 = (bf16[2,4,4,80,128]{4,3,2,1,0:T(8,128)(2,1)}, bf16[8,32,384]{2,1,0:T(8,128)(2,1)}) custom-call(bf16[16,8,768]{2,1,0:T(8,128)(2,1)} %bitcast.5, bf16[2,8,8,768]{3,2,1,0:T(8,128)(2,1)} %bitcast.6, bf16[2,8,96,96]{3,2,1,0:T(8,128)(2,1)} %refs_2_.1, f32[2,8,96]{2,1,0:T(8,128)} %refs_3_.1, bf16[2,8,96,96]{3,2,1,0:T(8,128)(2,1)} %refs_4_.1, ...), custom_call_target="tpu_custom_call" | custom-call | tf_op jit(solution)/shard_map/fused_filter/pallas_call | solution.py:650
  36.9 2.6 %unpack.1 = (f32[2,8,8,768]{3,2,1,0:T(8,128)}, f32[2,8,96,96]{3,2,1,0:T(8,128)}, f32[2,8,96]{2,1,0:T(8,128)}, f32[2,8,96,96]{3,2,1,0:T(8,128)}, f32[2,8,96]{2,1,0:T(8,128)}) custom-call(bf16[2,4,4,80,128]{4,3,2,1,0:T(8,128)(2,1)} %get-tuple-element.12.gather_hbm, bf16[8,32,384]{2,1,0:T(8,128)(2,1)} %get-tuple-element.13.arrived_hbm), custom_call_target="tpu_custom_call" | custom-call | tf_op jit(solution)/shard_map/unpack/pallas_call | solution.py:701

commit v4 on v3

--- a/solution.py
+++ b/solution.py
@@ -239,7 +239,10 @@
     m_local, k_local = filt_ref.shape[1:3]
     loads = [
         pltpu.make_async_copy(arrived_hbm, arrived_ref, sems.at[0]),
-        pltpu.make_async_copy(gather_hbm, gather_ref, sems.at[1]),
+    ] + [
+        pltpu.make_async_copy(gather_hbm.at[e, q], gather_ref.at[e, q], sems.at[12 + 2 * q + e])
+        for q in range(4)
+        for e in range(2)
     ]
     for load in loads:
         load.start()
@@ -254,8 +257,9 @@
                 filt_ref[p, half * (m_local // 2) + m] = whole[m * k_local : (m + 1) * k_local]
         stores.append(pltpu.make_async_copy(filt_ref.at[p], filt_hbm.at[p], sems.at[2 + p]))
         stores[-1].start()
-    loads[1].wait()
     for q in range(4):
+        loads[1 + 2 * q].wait()
+        loads[2 + 2 * q].wait()
         for b in range(blocks):
             piece = gather_ref[b % 2, q, b // 2].astype(f32)
             grad_ref[q, b, 0:keep, :] = piece[0:keep, 0:width]
@@ -283,6 +287,8 @@
     outer_off_hbm,
     cols_hbm,
     rows_hbm,
+    gather_out,
+    arrived_out,
     gather,
     recv_d,
     send_a,
@@ -606,6 +612,10 @@
         side_copy(side, source).start()
 
     exchange_recv(lon_copy, 2, send_d, recv_d, j, lons)
+    leaving = [pltpu.make_async_copy(recv_d, arrived_out, local_sem.at[10])]
+    leaving.append(pltpu.make_async_copy(gather.at[side], gather_out.at[side], local_sem.at[11]))
+    for store in leaving:
+        store.start()
     exchange_sent(lon_copy, 0, send_a, recv_a, j, lons)
     exchange_sent(lon_copy, 1, send_c, recv_c, j, lons)
     exchange_sent(lon_copy, 2, send_d, recv_d, j, lons)
@@ -620,6 +630,14 @@
         side_copy(side, q).wait_send()
     for q in range(lats):
         side_copy(1 - side, q).wait_recv()
+        leaving.append(
+            pltpu.make_async_copy(
+                gather.at[1 - side, q], gather_out.at[1 - side, q], local_sem.at[12 + q]
+            )
+        )
+        leaving[-1].start()
+    for store in leaving:
+        store.wait()
 
 
 def fused_device(fields, spec_cotangent, inner_kernel, inner_offset, outer_kernel, outer_offset):
@@ -638,7 +656,6 @@
     cols = jnp.asarray(column_tables(full_width, wavenumbers, lats))
     rows, unscale = row_tables(height, k_local)
     rows = jnp.asarray(rows)
-    vmem = pl.BlockSpec(memory_space=pltpu.VMEM)
     hbm = pl.BlockSpec(memory_space=pltpu.HBM)
     bf16, f32 = jnp.bfloat16, jnp.float32
     wide = (tokens, 2 * lanes)
@@ -657,8 +674,10 @@
             jax.ShapeDtypeStruct((blocks, part_rows // 2, 4 * width), bf16),
         ],
         in_specs=[hbm] * 8,
-        out_specs=[vmem] * 2,
+        out_specs=[hbm] * 2,
         scratch_shapes=[
+            pltpu.VMEM((2, lats, lons // 2, deep, lanes), bf16),
+            pltpu.VMEM((blocks, part_rows // 2, 4 * width), bf16),
             *pair(blocks, w_local, h_local * width),
             *pair(lats, h_local * k_local, 4 * width),
             *pair(blocks, part_rows // 2, 4 * width),
@@ -683,7 +702,7 @@
             dma((lons // 2, lats)),
             dma((lats,)),
             dma((lats,)),
-            dma((10,)),
+            dma((12 + lats,)),
         ],
         compiler_params=pltpu.CompilerParams(
             collective_id=0, has_side_effects=True, vmem_limit_bytes=63 * 1024 * 1024
@@ -716,7 +735,7 @@
             pltpu.VMEM((2, m_local, k_local, channels), f32),
             pltpu.VMEM((4, blocks, width, width), f32),
             pltpu.VMEM((4, blocks, width), f32),
-            dma((12,)),
+            dma((20,)),
         ],
         compiler_params=pltpu.CompilerParams(vmem_limit_bytes=63 * 1024 * 1024),
     )(gathered, arrived)

time: 39.6 us -> 39.4 us (level)
  no operation moved by 1% of the time
where the time goes in v4:
time: 39.4 us; the launch traced here: 39.3 us
  Pallas kernels  38.6 us (98%)
  between operations  0.64 us (2%)
    pallas_call x1, Pallas kernels, fused_device(): pl.pallas_call(lambda *refs: fused_kernel((lats, lons, blocks, width, lan...  36.1 us
    pallas_call x1, Pallas kernels, fused_device(): pl.pallas_call(unpack_kernel, name='unpack', out_shape=[jax.ShapeDtypeStr...  2.51 us

profile of v4, /device:TPU:0, one launch (start us, length us, event | category | flops | bytes accessed | tf_op | source)
XLA Modules:
  0.0 39.3 jit_solution(11810733895273956620)
XLA Ops:
  0.6 36.1 %fused_filter.1 = (bf16[2,4,4,80,128]{4,3,2,1,0:T(8,128)(2,1)}, bf16[8,32,384]{2,1,0:T(8,128)(2,1)}) custom-call(bf16[16,8,768]{2,1,0:T(8,128)(2,1)} %bitcast.5, bf16[2,8,8,768]{3,2,1,0:T(8,128)(2,1)} %bitcast.6, bf16[2,8,96,96]{3,2,1,0:T(8,128)(2,1)} %refs_2_.1, f32[2,8,96]{2,1,0:T(8,128)} %refs_3_.1, bf16[2,8,96,96]{3,2,1,0:T(8,128)(2,1)} %refs_4_.1, ...), custom_call_target="tpu_custom_call" | custom-call | tf_op jit(solution)/shard_map/fused_filter/pallas_call | solution.py:667
  36.8 2.5 %unpack.1 = (f32[2,8,8,768]{3,2,1,0:T(8,128)}, f32[2,8,96,96]{3,2,1,0:T(8,128)}, f32[2,8,96]{2,1,0:T(8,128)}, f32[2,8,96,96]{3,2,1,0:T(8,128)}, f32[2,8,96]{2,1,0:T(8,128)}) custom-call(bf16[2,4,4,80,128]{4,3,2,1,0:T(8,128)(2,1)} %get-tuple-element.12.gather_hbm, bf16[8,32,384]{2,1,0:T(8,128)(2,1)} %get-tuple-element.13.arrived_hbm), custom_call_target="tpu_custom_call" | custom-call | tf_op jit(solution)/shard_map/unpack/pallas_call | solution.py:720
